TPU v7x, 32 devices: a whole 2x2x4 slice. The times are simulated.
32 devices in a mesh: dp: 4 (over x, core), tensor: 8 (over z, y).
Axes of the slice: x: 2, y: 2, z: 4, core: 2. Of those that a mesh axis runs over, the one named last changes fastest.
Arguments:
- tokens: bfloat16 [8192, 2048], P(('dp', 'tensor')), may hold values from -6 to 6
- attn_gain: bfloat16 [2048], replicated, may hold values from 0.099609375 to 1.8984375
- w_query: bfloat16 [2048, 2048], P(None, 'tensor'), may hold values from -0.125 to 0.125
- w_key: bfloat16 [2048, 2048], P(None, 'tensor'), may hold values from -0.125 to 0.125
- w_value: bfloat16 [2048, 2048], P(None, 'tensor'), may hold values from -0.125 to 0.125
- conv_query: bfloat16 [4, 2048], P(None, 'tensor'), may hold values from -3 to 3
- conv_key: bfloat16 [4, 2048], P(None, 'tensor'), may hold values from -3 to 3
- conv_value: bfloat16 [4, 2048], P(None, 'tensor'), may hold values from -3 to 3
- w_beta: bfloat16 [2048, 16], P(None, 'tensor'), may hold values from -0.125 to 0.125
- w_gate_out: bfloat16 [2048, 2048], P(None, 'tensor'), may hold values from -0.125 to 0.125
- head_gain: bfloat16 [128], replicated, may hold values from 0.099609375 to 1.8984375
- w_out: bfloat16 [2048, 2048], P('tensor'), may hold values from -0.25 to 0.25
- ffn_gain: bfloat16 [2048], replicated, may hold values from 0.099609375 to 1.8984375
- w_gate: bfloat16 [2048, 5632], P(None, 'tensor'), may hold values from -0.125 to 0.125
- w_up: bfloat16 [2048, 5632], P(None, 'tensor'), may hold values from -0.125 to 0.125
- w_down: bfloat16 [5632, 2048], P('tensor'), may hold values from -0.15625 to 0.15625
- seq_starts: int32 [4, 2], P('dp'), may hold values from 0 to 1536, as said below
- seq_lengths: int32 [4, 2], P('dp'), may hold values from 512 to 1024, as said below
- cotangent: bfloat16 [8192, 2048], P(('dp', 'tensor')), may hold values from -6 to 6
Outputs:
- output: bfloat16 [8192, 2048], P(('dp', 'tensor'))
- grad_tokens: float32 [8192, 2048], P(('dp', 'tensor'))
- grad_attn_gain: float32 [2048], replicated
- grad_w_query: float32 [2048, 2048], P(None, 'tensor')
- grad_w_key: float32 [2048, 2048], P(None, 'tensor')
- grad_w_value: float32 [2048, 2048], P(None, 'tensor')
- grad_conv_query: float32 [4, 2048], P(None, 'tensor')
- grad_conv_key: float32 [4, 2048], P(None, 'tensor')
- grad_conv_value: float32 [4, 2048], P(None, 'tensor')
- grad_w_beta: float32 [2048, 16], P(None, 'tensor')
- grad_w_gate_out: float32 [2048, 2048], P(None, 'tensor')
- grad_head_gain: float32 [128], replicated
- grad_w_out: float32 [2048, 2048], P('tensor')
- grad_ffn_gain: float32 [2048], replicated
- grad_w_gate: float32 [2048, 5632], P(None, 'tensor')
- grad_w_up: float32 [2048, 5632], P(None, 'tensor')
- grad_w_down: float32 [5632, 2048], P('tensor')
Inputs may be any that keep to these rules, and one draw needn't show every extreme that they name: `seq_lengths`: each shard holds 2 sequences; the first shard's first sequence has 1024 tokens and its last one 2048 // 4. `seq_starts`: the sequences of a shard lie in order within its 2048 slots and do not intersect, the first starting at slot 0; the other slots are padding. The first shard's last sequence ends at its last slot.
All inputs are finite; a program needn't handle non-finite values.
Results may differ from a plain program's by a relative error of at most 0.02.
Values may be sent and summed in bfloat16 or wider, within the bound.
A program may use at most 320 MiB of HBM per device.

v0:
```python
import jax
import jax.numpy as jnp
from jax import lax
from jax.sharding import PartitionSpec as P

STRETCH = 64
highest = lax.Precision.HIGHEST


def round_pass(value):
    return lax.optimization_barrier(value.astype(jnp.bfloat16)).astype(jnp.float32)


def round_keep(value):
    return (round_pass(value), None)


def round_grad(kept, grad):
    return (grad,)


def make_rounding():
    rounder = jax.custom_vjp(round_pass)
    rounder.defvjp(round_keep, round_grad)
    return rounder


def positions(starts, lengths, slot_count):
    places = jnp.arange(slot_count, dtype=jnp.int32)
    begun = (places[:, None] >= starts[None, :]).astype(jnp.int32)
    ended = (places[:, None] >= (starts + lengths)[None, :]).astype(jnp.int32)
    segment = jnp.sum(begun + ended, axis=1)
    live = (segment % 2).astype(jnp.float32)
    return (segment, live)


def short_conv(inputs, taps, segment):
    result = inputs * taps[0]
    for offset in range(1, taps.shape[0]):
        moved = jnp.concatenate(
            [jnp.zeros((offset, inputs.shape[1]), jnp.float32), inputs[:-offset]], 0
        )
        earlier = jnp.concatenate([jnp.full((offset,), -1, jnp.int32), segment[:-offset]], 0)
        result = result + moved * taps[offset] * (earlier == segment).astype(jnp.float32)[:, None]
    return result


def unit_rows(inputs):
    return inputs * lax.rsqrt(jnp.sum(inputs * inputs, axis=-1, keepdims=True) + 1e-06)


def delta_rule(queries, key_rows, values, strength, segment):
    slot_count, head_width = queries.shape
    blocks = slot_count // STRETCH
    query_blocks = (queries * head_width ** (-0.5)).reshape(blocks, STRETCH, head_width)
    key_blocks = key_rows.reshape(blocks, STRETCH, head_width)
    value_blocks = values.reshape(blocks, STRETCH, head_width)
    beta_blocks = strength.reshape(blocks, STRETCH)
    seg_blocks = segment.reshape(blocks, STRETCH)
    same_seg = (seg_blocks[:, :, None] == seg_blocks[:, None, :]).astype(jnp.float32)
    places = jnp.arange(STRETCH)
    strict = (places[:, None] > places[None, :]).astype(jnp.float32)
    inclusive = (places[:, None] >= places[None, :]).astype(jnp.float32)
    key_inner = jnp.einsum("nik,njk->nij", key_blocks, key_blocks, precision=highest)
    system = (
        jnp.eye(STRETCH, dtype=jnp.float32)[None]
        + beta_blocks[:, :, None] * key_inner * same_seg * strict
    )
    weighted = lax.linalg.triangular_solve(
        system, beta_blocks[:, :, None] * key_blocks, left_side=True, lower=True, unit_diagonal=True
    )
    updates = lax.linalg.triangular_solve(
        system,
        beta_blocks[:, :, None] * value_blocks,
        left_side=True,
        lower=True,
        unit_diagonal=True,
    )
    within = (
        jnp.einsum("nik,njk->nij", query_blocks, key_blocks, precision=highest)
        * same_seg
        * inclusive
    )
    earlier_last = jnp.concatenate([jnp.full((1,), -1, jnp.int32), seg_blocks[:-1, STRETCH - 1]], 0)
    continued = (seg_blocks[:, 0] == earlier_last).astype(jnp.float32)
    carried = same_seg[:, :, 0] * continued[:, None]
    ending = same_seg[:, :, STRETCH - 1]
    kept_state = continued * same_seg[:, 0, STRETCH - 1]

    def advance(memory, pieces):
        query_part, key_part, weight_part, update_part, mixing, carry_part, end_part, keep_part = (
            pieces
        )
        change = update_part - carry_part[:, None] * jnp.dot(
            weight_part, memory.T, precision=highest
        )
        result = carry_part[:, None] * jnp.dot(query_part, memory.T, precision=highest) + jnp.dot(
            mixing, change, precision=highest
        )
        memory = keep_part * memory + jnp.dot(
            (end_part[:, None] * change).T, key_part, precision=highest
        )
        return (memory, result)

    start_memory = jnp.zeros((head_width, head_width), jnp.float32)
    last_memory, outputs = lax.scan(
        jax.checkpoint(advance),
        start_memory,
        (query_blocks, key_blocks, weighted, updates, within, carried, ending, kept_state),
    )
    return outputs.reshape(slot_count, head_width)


def mixer_local(
    proj_query,
    proj_key,
    proj_value,
    proj_beta,
    proj_gate,
    taps_query,
    taps_key,
    taps_value,
    gain_head,
    segment,
    live,
    rounder,
):
    slot_count = proj_query.shape[0]
    head_count = proj_beta.shape[1]
    head_width = proj_query.shape[1] // head_count

    def feature(projected, taps):
        return jax.nn.silu(short_conv(projected, taps, segment)).reshape(
            slot_count, head_count, head_width
        )

    queries = rounder(unit_rows(feature(proj_query, taps_query)))
    key_rows = rounder(unit_rows(feature(proj_key, taps_key)))
    values = rounder(feature(proj_value, taps_value))
    strength = jax.nn.sigmoid(proj_beta)
    delta_out = jax.vmap(delta_rule, in_axes=(1, 1, 1, 1, None), out_axes=1)(
        queries, key_rows, values, strength, segment
    )
    head_normed = (
        delta_out
        * lax.rsqrt(jnp.mean(delta_out * delta_out, axis=-1, keepdims=True) + 1e-05)
        * gain_head
    )
    gated = (
        head_normed
        * jax.nn.silu(proj_gate.reshape(slot_count, head_count, head_width))
        * live[:, None, None]
    )
    return gated.reshape(slot_count, head_count * head_width)


def norm_back(inputs, scale, gain, grad_normed):
    weighted_grad = gain * grad_normed
    inner = jnp.mean(weighted_grad * inputs, axis=1, keepdims=True)
    grad_inputs = scale * weighted_grad - inputs * scale * scale * scale * inner
    grad_gain = jnp.sum(grad_normed * inputs * scale, axis=0)
    return (grad_inputs, grad_gain)


def shards(
    tokens,
    attn_gain,
    w_query,
    w_key,
    w_value,
    conv_query,
    conv_key,
    conv_value,
    w_beta,
    w_gate_out,
    head_gain,
    w_out,
    ffn_gain,
    w_gate,
    w_up,
    w_down,
    seq_starts,
    seq_lengths,
    cotangent,
):
    row_count = tokens.shape[0]
    slot_count = row_count * lax.axis_size("tensor")
    segment, live = positions(seq_starts[0], seq_lengths[0], slot_count)
    rounder = make_rounding()
    inputs = tokens.astype(jnp.float32)
    gain_first = attn_gain.astype(jnp.float32)
    scale_first = lax.rsqrt(jnp.mean(inputs * inputs, axis=1, keepdims=True) + 1e-06)
    normed = (inputs * scale_first * gain_first).astype(jnp.bfloat16)
    normed_full = lax.all_gather(normed, "tensor", axis=0, tiled=True)
    mixer_weights = (w_query, w_key, w_value, w_beta, w_gate_out)
    projected = [
        jnp.dot(normed_full, weight, preferred_element_type=jnp.float32) for weight in mixer_weights
    ]

    def mixer_piece(
        proj_query,
        proj_key,
        proj_value,
        proj_beta,
        proj_gate,
        taps_query,
        taps_key,
        taps_value,
        gain_head,
    ):
        return mixer_local(
            proj_query,
            proj_key,
            proj_value,
            proj_beta,
            proj_gate,
            taps_query,
            taps_key,
            taps_value,
            gain_head,
            segment,
            live,
            rounder,
        )

    mixed, mixer_pullback = jax.vjp(
        mixer_piece,
        projected[0],
        projected[1],
        projected[2],
        projected[3],
        projected[4],
        conv_query.astype(jnp.float32),
        conv_key.astype(jnp.float32),
        conv_value.astype(jnp.float32),
        head_gain.astype(jnp.float32),
    )
    mixed_low = mixed.astype(jnp.bfloat16)
    attended = lax.psum_scatter(
        jnp.dot(mixed_low, w_out, preferred_element_type=jnp.float32).astype(jnp.bfloat16),
        "tensor",
        scatter_dimension=0,
        tiled=True,
    ).astype(jnp.float32)
    resid = inputs + attended
    gain_second = ffn_gain.astype(jnp.float32)
    scale_second = lax.rsqrt(jnp.mean(resid * resid, axis=1, keepdims=True) + 1e-06)
    ffn_in = (resid * scale_second * gain_second).astype(jnp.bfloat16)
    ffn_full = lax.all_gather(ffn_in, "tensor", axis=0, tiled=True)
    gate_pre = jnp.dot(ffn_full, w_gate, preferred_element_type=jnp.float32)
    up_pre = jnp.dot(ffn_full, w_up, preferred_element_type=jnp.float32)
    sigmoid_gate = jax.nn.sigmoid(gate_pre)
    silu_gate = gate_pre * sigmoid_gate
    hidden = (silu_gate * up_pre).astype(jnp.bfloat16)
    output = resid + lax.psum_scatter(
        jnp.dot(hidden, w_down, preferred_element_type=jnp.float32).astype(jnp.bfloat16),
        "tensor",
        scatter_dimension=0,
        tiled=True,
    ).astype(jnp.float32)
    grad_full = lax.all_gather(cotangent, "tensor", axis=0, tiled=True)
    grad_hidden = jnp.einsum("sd,fd->sf", grad_full, w_down, preferred_element_type=jnp.float32)
    grad_w_down = jnp.einsum("sf,sd->fd", hidden, grad_full, preferred_element_type=jnp.float32)
    grad_gate = (
        grad_hidden * up_pre * sigmoid_gate * (1.0 + gate_pre * (1.0 - sigmoid_gate))
    ).astype(jnp.bfloat16)
    grad_up = (grad_hidden * silu_gate).astype(jnp.bfloat16)
    grad_w_gate = jnp.einsum("sd,sf->df", ffn_full, grad_gate, preferred_element_type=jnp.float32)
    grad_w_up = jnp.einsum("sd,sf->df", ffn_full, grad_up, preferred_element_type=jnp.float32)
    grad_ffn_in = lax.psum_scatter(
        (
            jnp.einsum("sf,df->sd", grad_gate, w_gate, preferred_element_type=jnp.float32)
            + jnp.einsum("sf,df->sd", grad_up, w_up, preferred_element_type=jnp.float32)
        ).astype(jnp.bfloat16),
        "tensor",
        scatter_dimension=0,
        tiled=True,
    ).astype(jnp.float32)
    grad_through, grad_ffn_gain = norm_back(resid, scale_second, gain_second, grad_ffn_in)
    grad_resid = cotangent.astype(jnp.float32) + grad_through
    grad_attended = lax.all_gather(grad_resid.astype(jnp.bfloat16), "tensor", axis=0, tiled=True)
    grad_mixed = jnp.einsum("sd,hd->sh", grad_attended, w_out, preferred_element_type=jnp.float32)
    grad_w_out = jnp.einsum(
        "sh,sd->hd", mixed_low, grad_attended, preferred_element_type=jnp.float32
    )
    pulled = mixer_pullback(grad_mixed)
    grad_projected = [pulled[index].astype(jnp.bfloat16) for index in range(5)]
    grad_mixer_weights = [
        jnp.einsum("sd,sh->dh", normed_full, grad_part, preferred_element_type=jnp.float32)
        for grad_part in grad_projected
    ]
    summed = jnp.zeros((row_count * lax.axis_size("tensor"), normed.shape[1]), jnp.float32)
    for grad_part, weight in zip(grad_projected, mixer_weights):
        summed = summed + jnp.einsum(
            "sh,dh->sd", grad_part, weight, preferred_element_type=jnp.float32
        )
    grad_normed = lax.psum_scatter(
        summed.astype(jnp.bfloat16), "tensor", scatter_dimension=0, tiled=True
    ).astype(jnp.float32)
    grad_first, grad_attn_gain = norm_back(inputs, scale_first, gain_first, grad_normed)
    grad_tokens = grad_resid + grad_first
    grad_attn_gain, grad_ffn_gain, grad_head_gain = lax.psum(
        (grad_attn_gain, grad_ffn_gain, pulled[8]), ("dp", "tensor")
    )
    mixer_grads = (
        grad_mixer_weights[0],
        grad_mixer_weights[1],
        grad_mixer_weights[2],
        pulled[5],
        pulled[6],
        pulled[7],
        grad_mixer_weights[3],
        grad_mixer_weights[4],
        grad_w_out,
    )
    summed_all = (
        lax.psum(mixer_grads[0].astype(jnp.bfloat16), "dp").astype(jnp.float32),
        lax.psum(mixer_grads[1].astype(jnp.bfloat16), "dp").astype(jnp.float32),
        lax.psum(mixer_grads[2].astype(jnp.bfloat16), "dp").astype(jnp.float32),
        lax.psum(mixer_grads[3].astype(jnp.bfloat16), "dp").astype(jnp.float32),
        lax.psum(mixer_grads[4].astype(jnp.bfloat16), "dp").astype(jnp.float32),
        lax.psum(mixer_grads[5].astype(jnp.bfloat16), "dp").astype(jnp.float32),
        lax.psum(mixer_grads[6].astype(jnp.bfloat16), "dp").astype(jnp.float32),
        lax.psum(mixer_grads[7].astype(jnp.bfloat16), "dp").astype(jnp.float32),
        lax.psum(mixer_grads[8].astype(jnp.bfloat16), "dp").astype(jnp.float32),
        lax.psum(grad_w_gate.astype(jnp.bfloat16), "dp").astype(jnp.float32),
        lax.psum(grad_w_up.astype(jnp.bfloat16), "dp").astype(jnp.float32),
        lax.psum(grad_w_down.astype(jnp.bfloat16), "dp").astype(jnp.float32),
    )
    mixer_grads = summed_all[:9]
    grad_w_gate, grad_w_up, grad_w_down = (summed_all[9], summed_all[10], summed_all[11])
    return (
        output.astype(jnp.bfloat16),
        grad_tokens,
        grad_attn_gain,
        mixer_grads[0],
        mixer_grads[1],
        mixer_grads[2],
        mixer_grads[3],
        mixer_grads[4],
        mixer_grads[5],
        mixer_grads[6],
        mixer_grads[7],
        grad_head_gain,
        mixer_grads[8],
        grad_ffn_gain,
        grad_w_gate,
        grad_w_up,
        grad_w_down,
    )


def solution(mesh):
    placed = (
        P(("dp", "tensor"), None),
        P(),
        P(None, "tensor"),
        P(None, "tensor"),
        P(None, "tensor"),
        P(None, "tensor"),
        P(None, "tensor"),
        P(None, "tensor"),
        P(None, "tensor"),
        P(None, "tensor"),
        P(),
        P("tensor", None),
        P(),
        P(None, "tensor"),
        P(None, "tensor"),
        P("tensor", None),
        P("dp", None),
        P("dp", None),
        P(("dp", "tensor"), None),
    )
    return jax.shard_map(
        shards,
        mesh=mesh,
        in_specs=placed,
        out_specs=(
            P(("dp", "tensor"), None),
            P(("dp", "tensor"), None),
            P(),
            P(None, "tensor"),
            P(None, "tensor"),
            P(None, "tensor"),
            P(None, "tensor"),
            P(None, "tensor"),
            P(None, "tensor"),
            P(None, "tensor"),
            P(None, "tensor"),
            P(),
            P("tensor", None),
            P(),
            P(None, "tensor"),
            P(None, "tensor"),
            P("tensor", None),
        ),
        check_vma=False,
    )
```

profile of v0, /device:TPU:0, one launch (start us, length us, event | category | flops | bytes accessed | tf_op | source)
XLA Modules:
  0.0 2470.4 jit_solution(2814759676212930123)
XLA Ops:
  21.9 118.7 %all-gather.5.cloned.1.call-done = bf16[2048,2048]{1,0:T(8,128)(2,1)} async-done(((bf16[256,2048]{1,0:T(8,128)(2,1)}), bf16[2048,2048]{1,0:T(8,128)(2,1)}) %all-gather.5.cloned.1.call-update) | async-done | bytes 8388624 | tf_op jit(solution)/shard_map/all_gather | solution.py:194
  224.4 9.4 multiply_bitcast_fusion
  233.7 134.0 %custom-call.14 = f32[2,32,1,64,64]{1,3,4,2,0:T(8,128)} custom-call(f32[2,32,1,64,64]{1,4,3,2,0:T(8,128)} %get-tuple-element.855), custom_call_target="InvertDiagBlocksLowerTriangular" | custom-call | tf_op jit(solution)/shard_map/jvp(vmap())/triangular_solve/custom-call.1 | solution.py:72
  389.4 235.3 %while.40 = (s32[]{:T(128)}, f32[2,128,128]{2,1,0:T(8,128)S(1)}, f32[32,2,64,128]{3,2,0,1:T(8,128)}, f32[32,2,128,128]{3,2,1,0:T(8,128)}, f32[32]{0:T(128)S(1)},...) while((s32[]{:T(128)}, f32[2,128,128]{2,1,0:T(8,128)S(1)}, ...), condition=%wide.region_5.7_spmd.clone, body=%wide.region_4.6_spmd.clone.sunk | while | flops 88358912 | bytes 1512373 | solution.py:106
  640.4 146.7 %reduce-scatter.5.cloned.1.call-done = bf16[256,2048]{1,0:T(8,128)(2,1)} async-done(((bf16[2048,2048]{1,0:T(8,128)(2,1)}), bf16[256,2048]{1,0:T(8,128)(2,1)}) %reduce-scatter.5.cloned.1.call-update) | async-done | bytes 1048592 | tf_op jit(solution)/shard_map/reduce_scatter | solution.py:239
  791.4 123.5 %all-gather.7.cloned.1.call-done = bf16[2048,2048]{1,0:T(8,128)(2,1)} async-done(((bf16[256,2048]{1,0:T(8,128)(2,1)}), bf16[2048,2048]{1,0:T(8,128)(2,1)}) %all-gather.7.cloned.1.call-update) | async-done | bytes 8388624 | tf_op jit(solution)/shard_map/all_gather | solution.py:249
  914.9 11.4 fusion.142
  934.2 106.0 %all-gather.9.cloned.1.call-done = bf16[2048,2048]{1,0:T(8,128)(2,1)} async-done(((bf16[256,2048]{1,0:T(8,128)(2,1)}), bf16[2048,2048]{1,0:T(8,128)(2,1)}) %all-gather.9.cloned.1.call-update) | async-done | bytes 8388624 | tf_op jit(solution)/shard_map/all_gather | solution.py:261
  1040.2 14.7 multiply_convert_fusion
  1054.9 10.7 fusion.143
  1065.6 12.5 add_convert_fusion.1
  1078.2 147.3 %reduce-scatter.9.cloned.1.call-done = bf16[256,2048]{1,0:T(8,128)(2,1)} async-done(((bf16[2048,2048]{1,0:T(8,128)(2,1)}), bf16[256,2048]{1,0:T(8,128)(2,1)}) %reduce-scatter.9.cloned.1.call-update) | async-done | bytes 1048592 | tf_op jit(solution)/shard_map/reduce_scatter | solution.py:270
  1245.1 10.7 convolution_convert_fusion.2
  1255.9 11.0 convolution_convert_fusion.3
  1274.4 82.0 %all-gather.11.cloned.1.call-done = bf16[2048,2048]{1,0:T(8,128)(2,1)} async-done(((bf16[256,2048]{1,0:T(8,128)(2,1)}), bf16[2048,2048]{1,0:T(8,128)(2,1)}) %all-gather.11.cloned.1.call-update) | async-done | bytes 8388624 | tf_op jit(solution)/shard_map/all_gather | solution.py:281
  1382.8 377.5 %while.41 = (s32[]{:T(128)}, f32[2,128,128]{2,1,0:T(8,128)S(1)}, f32[32,2,64,128]{3,2,0,1:T(8,128)}, f32[32,2,64,128]{3,2,0,1:T(8,128)}, f32[32,2,64,128]{3,2,1,...) while((s32[]{:T(128)}, f32[2,128,128]{2,1,0:T(8,128)S(1)}, ...), condition=%wide.region_14.16_spmd.clone, body=%wide.region_13.15_spmd.clone.sunk | while | flops 201637888 | bytes 3902479 | solution.py:106
  1824.4 10.2 fusion.79
  1942.7 26.4 %add_convert_fusion = bf16[2048,2048]{1,0:T(8,128)(2,1)} fusion(f32[2048,2048]{1,0:T(8,128)} %fusion.133, f32[2048,2048]{1,0:T(8,128)} %fusion.151, f32[2048,2048]{1,0:T(8,128)} %fusion.145, f32[2048,2048]{1,0:T(8,128)} %fusion.150, bf16[2048,256]{0,1:T(8,128)(2,1)S(1)} %bitcast.470, bf16[2048,256]{1,0:T(8,128)(2,1)S(1)} %copy-done.58), kind=kOutput, calls=%fused_computation.70 | convolution fusion | flops 2168455168 | bytes 77594624 | tf_op jit(solution)/shard_map/sh,dh->sd/dot_general | solution.py:294
  1969.4 10.9 convolution_convert_fusion
  1985.1 12.4 all-reduce.33
  1999.9 151.3 %all-reduce.37.cloned.1.call-done = (bf16[2048,256]{1,0:T(8,128)(2,1)}, bf16[2048,256]{1,0:T(8,128)(2,1)}, bf16[2048,256]{1,0:T(8,128)(2,1)}, bf16[2048,256]{1,0...) async-done(((bf16[2048,256]{1,0:T(8,128)(2,1)}, bf16[2048,256]{1,0:T(8,128)(2,1)}, ...) | async-done | bytes 13893648 | tf_op jit(solution)/shard_map/psum | solution.py:317
  2171.1 133.0 %reduce-scatter.11.cloned.1.call-done = bf16[256,2048]{1,0:T(8,128)(2,1)} async-done(((bf16[2048,2048]{1,0:T(8,128)(2,1)}), bf16[256,2048]{1,0:T(8,128)(2,1)}) %reduce-scatter.11.cloned.1.call-update) | async-done | bytes 1048592 | tf_op jit(solution)/shard_map/reduce_scatter | solution.py:297
  2306.3 43.1 %all-reduce.32 = (f32[2048]{0:T(1024)}, f32[128]{0:T(128)}, f32[2048]{0:T(1024)}) all-reduce(f32[2048]{0:T(1024)S(1)} %get-tuple-element.718, f32[128]{0:T(128)S(1)} %copy-done.130, f32[2048]{0:T(1024)S(1)} %copy-done.95), channel_id=1, replica_groups=mesh['dp'=4,'tensor'=8] {'dp','tensor'}, use_global_device_ids=true, to_apply=%region_23.27 | all-reduce | flops 4224 | bytes 33792 | tf_op jit(solution)/shard_map/psum | solution.py:302
  2349.5 107.7 %reduce-scatter.7.cloned.1.call-done = bf16[256,2048]{1,0:T(8,128)(2,1)} async-done(((bf16[2048,2048]{1,0:T(8,128)(2,1)}), bf16[256,2048]{1,0:T(8,128)(2,1)}) %reduce-scatter.7.cloned.1.call-update) | async-done | bytes 1048592 | tf_op jit(solution)/shard_map/reduce_scatter | solution.py:255
  (1239 shorter events, 1018.0 us)
Async XLA Ops:
  7.2 1033.0 %copy-start = (bf16[704,2048]{1,0:T(8,128)(2,1)S(1)}, bf16[704,2048]{1,0:T(8,128)(2,1)}, u32[]{:S(2)}) copy-start(bf16[704,2048]{1,0:T(8,128)(2,1)} %param.44) | copy-start | bytes 8650756
  7.2 133.3 %all-gather.5.cloned.1.call-start = ((), (), s32[]{:S(2)}) async-start(), calls=%async_computation.4 | async-start | bytes 9437184 | tf_op jit(solution)/shard_map/all_gather | solution.py:194
  12.8 774.3 %reduce-scatter.5.cloned.1.call-start = ((), (), s32[]{:S(2)}) async-start(), calls=%async_computation.5 | async-start | bytes 9437184 | tf_op jit(solution)/shard_map/reduce_scatter | solution.py:239
  19.5 204.8 %copy-start.69 = (f32[64,64]{1,0:T(8,128)}, f32[64,64]{1,0:T(8,128)S(1)}, u32[]{:S(2)}) copy-start(f32[64,64]{1,0:T(8,128)S(1)} %fusion.110) | copy-start | bytes 49156
  19.5 204.8 %copy-start.73 = (f32[64,64]{1,0:T(8,128)}, f32[64,64]{1,0:T(8,128)S(1)}, u32[]{:S(2)}) copy-start(f32[64,64]{1,0:T(8,128)S(1)} %fusion.109) | copy-start | bytes 49156
  20.0 163.9 %copy-start.102 = (f32[1,256]{1,0:T(1,128)}, f32[1,256]{1,0:T(1,128)S(1)}, u32[]{:S(2)}) copy-start(f32[1,256]{1,0:T(1,128)S(1)} %get-tuple-element.879) | copy-start | bytes 3076
  20.0 163.9 %copy-start.106 = (f32[1,256]{1,0:T(1,128)}, f32[1,256]{1,0:T(1,128)S(1)}, u32[]{:S(2)}) copy-start(f32[1,256]{1,0:T(1,128)S(1)} %get-tuple-element.881) | copy-start | bytes 3076
  20.0 163.9 %copy-start.108 = (f32[1,256]{1,0:T(1,128)}, f32[1,256]{1,0:T(1,128)S(1)}, u32[]{:S(2)}) copy-start(f32[1,256]{1,0:T(1,128)S(1)} %get-tuple-element.880) | copy-start | bytes 3076
  20.0 163.9 %copy-start.120 = (f32[1,256]{1,0:T(1,128)}, f32[1,256]{1,0:T(1,128)S(1)}, u32[]{:S(2)}) copy-start(f32[1,256]{1,0:T(1,128)S(1)} %get-tuple-element.882) | copy-start | bytes 3076
  20.0 163.8 %copy-start.104 = (f32[1,256]{1,0:T(1,128)}, f32[1,256]{1,0:T(1,128)S(1)}, u32[]{:S(2)}) copy-start(f32[1,256]{1,0:T(1,128)S(1)} %get-tuple-element.887) | copy-start | bytes 3076
  20.2 204.1 %copy-start.91 = (pred[64,64]{1,0:T(8,128)(4,1)}, pred[64,64]{1,0:T(8,128)(4,1)S(1)}, u32[]{:S(2)}) copy-start(pred[64,64]{1,0:T(8,128)(4,1)S(1)} %iota_compare_fusion.1) | copy-start | bytes 12292
  146.9 230.8 %copy-start.56 = (f32[2,32,64]{2,1,0:T(8,128)}, f32[2,32,64]{2,1,0:T(8,128)S(1)}, u32[]{:S(2)}) copy-start(f32[2,32,64]{2,1,0:T(8,128)S(1)} %mul.1002) | copy-start | bytes 49156
  639.8 275.1 %all-gather.7.cloned.1.call-start = ((), (), s32[]{:S(2)}) async-start(), calls=%async_computation.6 | async-start | bytes 9437184 | tf_op jit(solution)/shard_map/all_gather | solution.py:249
  640.4 588.5 %copy-start.75 = (f32[2048]{0:T(1024)}, f32[2048]{0:T(1024)S(1)}, u32[]{:S(2)}) copy-start(f32[2048]{0:T(1024)S(1)} %convert_element_type.274) | copy-start | bytes 24580
  789.3 439.6 %copy-start.96 = (f32[256]{0:T(256)}, f32[256]{0:T(256)S(1)}, u32[]{:S(2)}) copy-start(f32[256]{0:T(256)S(1)} %add_rsqrt_fusion.2) | copy-start | bytes 3076
  790.8 249.4 %all-gather.9.cloned.1.call-start = ((), (), s32[]{:S(2)}) async-start(), calls=%async_computation.8 | async-start | bytes 9437184 | tf_op jit(solution)/shard_map/all_gather | solution.py:261
  791.4 434.2 %reduce-scatter.9.cloned.1.call-start = ((), (), s32[]{:S(2)}) async-start(), calls=%async_computation.9 | async-start | bytes 9437184 | tf_op jit(solution)/shard_map/reduce_scatter | solution.py:270
  1078.2 278.2 %all-gather.11.cloned.1.call-start = ((), (), s32[]{:S(2)}) async-start(), calls=%async_computation.10 | async-start | bytes 9437184 | tf_op jit(solution)/shard_map/all_gather | solution.py:281
  1232.3 918.9 %all-reduce.37.cloned.1.call-start = ((), (), s32[]{:S(2)}) async-start(), calls=%async_computation.12 | async-start | bytes 27787264 | tf_op jit(solution)/shard_map/psum | solution.py:317
  1908.3 395.8 %reduce-scatter.11.cloned.1.call-start = ((), (), s32[]{:S(2)}) async-start(), calls=%async_computation.11 | async-start | bytes 9437184 | tf_op jit(solution)/shard_map/reduce_scatter | solution.py:297
  1969.1 488.0 %reduce-scatter.7.cloned.1.call-start = ((), (), s32[]{:S(2)}) async-start(), calls=%async_computation.7 | async-start | bytes 9437184 | tf_op jit(solution)/shard_map/reduce_scatter | solution.py:255
  2171.1 286.1 %copy-start.76 = (f32[2048]{0:T(1024)S(1)}, f32[2048]{0:T(1024)}, u32[]{:S(2)}) copy-start(f32[2048]{0:T(1024)} %copy-done.75) | copy-start | bytes 24580
  2171.1 286.1 %copy-start.97 = (f32[256]{0:T(256)S(1)}, f32[256]{0:T(256)}, u32[]{:S(2)}) copy-start(f32[256]{0:T(256)} %copy-done.96) | copy-start | bytes 3076
  2171.1 286.1 %copy-start.101 = (f32[256]{0:T(256)S(1)}, f32[256]{0:T(256)}, u32[]{:S(2)}) copy-start(f32[256]{0:T(256)} %copy-done.100) | copy-start | bytes 3076
  (131 other events, 2880.6 us)
Sparse Core Ops, SparseCore 0:
  12.9 127.6 all-gather.4
  639.9 147.1 reduce-scatter.4
  790.9 123.9 all-gather.6
  917.1 123.1 all-gather.8
  1078.3 147.2 reduce-scatter.8
  1232.4 123.9 all-gather.10
  1908.4 242.8 all-reduce.36
  2154.9 149.1 reduce-scatter.10
  2308.2 148.9 reduce-scatter.6
where the time goes:
time: 2490 us; the launch traced here: 2470 us
  waiting for transfers between devices  1120 us (45%)
  matrix products  695 us (28%)
  local copies, waits for them, and re-layouts  292 us (12%)
  other arithmetic  292 us (12%)
  blocking collectives  55.6 us (2%)
    psum x1, waiting for transfers between devices, shards(): lax.psum(mixer_grads[0].astype(jnp.bfloat16), 'dp').astype(jnp.float32)  151 us
    reduce_scatter x1, waiting for transfers between devices, shards(): lax.psum_scatter((jnp.einsum('sf,df->sd', grad_gate, w_gate, preferred_el...  147 us
    reduce_scatter x1, waiting for transfers between devices, shards(): lax.psum_scatter(jnp.dot(mixed_low, w_out, preferred_element_type=jnp.flo...  147 us
    squeeze x192, local copies, waits for them, and re-layouts, delta_rule(): lax.scan(jax.checkpoint(advance), start_memory, (query_blocks, key_blocks...  141 us
    another operation x4, other arithmetic, delta_rule(): lax.linalg.triangular_solve(system, beta_blocks[:, :, None] * value_block...  134 us
    reduce_scatter x1, waiting for transfers between devices, shards(): lax.psum_scatter(summed.astype(jnp.bfloat16), 'tensor', scatter_dimension...  133 us
    all_gather x1, waiting for transfers between devices, shards(): ffn_full = lax.all_gather(ffn_in, 'tensor', axis=0, tiled=True)  123 us
    all_gather x1, waiting for transfers between devices, shards(): normed_full = lax.all_gather(normed, 'tensor', axis=0, tiled=True)  119 us
  transfers between devices with their start and end apart: 9, of which 9 were waited for; matrix products, arithmetic and copies ran while one was open for 7% of the time, Pallas kernels for 0%

commit v1 on v0

--- a/solution.py
+++ b/solution.py
@@ -5,6 +5,10 @@
 
 STRETCH = 64
 highest = lax.Precision.HIGHEST
+
+
+def process_strings_here(u, along_axis):
+    return lax.all_gather(u, along_axis).sum(axis=0)
 
 
 def round_pass(value):
@@ -314,7 +318,7 @@
         grad_w_out,
     )
     summed_all = (
-        lax.psum(mixer_grads[0].astype(jnp.bfloat16), "dp").astype(jnp.float32),
+        process_strings_here(mixer_grads[0].astype(jnp.bfloat16), "dp").astype(jnp.float32),
         lax.psum(mixer_grads[1].astype(jnp.bfloat16), "dp").astype(jnp.float32),
         lax.psum(mixer_grads[2].astype(jnp.bfloat16), "dp").astype(jnp.float32),
         lax.psum(mixer_grads[3].astype(jnp.bfloat16), "dp").astype(jnp.float32),

time: 2490 us -> 2490 us (level)
  transfers between devices with their start and end apart: 9 -> 10, of which waited for: 9 -> 9; matrix products, arithmetic and copies ran while one was open for 7% -> 8% of each run, Pallas kernels for 0% -> 0%
where the time goes in v1:
time: 2490 us; the launch traced here: 2460 us
  waiting for transfers between devices  1100 us (44%)
  matrix products  695 us (28%)
  local copies, waits for them, and re-layouts  300 us (12%)
  other arithmetic  294 us (12%)
  blocking collectives  55.5 us (2%)
    reduce_scatter x1, waiting for transfers between devices, shards(): lax.psum_scatter((jnp.einsum('sf,df->sd', grad_gate, w_gate, preferred_el...  147 us
    reduce_scatter x1, waiting for transfers between devices, shards(): lax.psum_scatter(jnp.dot(mixed_low, w_out, preferred_element_type=jnp.flo...  147 us
    squeeze x192, local copies, waits for them, and re-layouts, delta_rule(): lax.scan(jax.checkpoint(advance), start_memory, (query_blocks, key_blocks...  141 us
    reduce_scatter x1, waiting for transfers between devices, shards(): lax.psum_scatter(summed.astype(jnp.bfloat16), 'tensor', scatter_dimension...  134 us
    another operation x4, other arithmetic, delta_rule(): lax.linalg.triangular_solve(system, beta_blocks[:, :, None] * value_block...  134 us
    psum x1, waiting for transfers between devices, shards(): lax.psum(mixer_grads[1].astype(jnp.bfloat16), 'dp').astype(jnp.float32)  134 us
    all_gather x1, waiting for transfers between devices, shards(): ffn_full = lax.all_gather(ffn_in, 'tensor', axis=0, tiled=True)  123 us
    all_gather x1, waiting for transfers between devices, shards(): normed_full = lax.all_gather(normed, 'tensor', axis=0, tiled=True)  119 us
  transfers between devices with their start and end apart: 10, of which 9 were waited for; matrix products, arithmetic and copies ran while one was open for 8% of the time, Pallas kernels for 0%

profile of v1, /device:TPU:0, one launch (start us, length us, event | category | flops | bytes accessed | tf_op | source)
XLA Modules:
  0.0 2464.9 jit_solution(8878827422464059386)
XLA Ops:
  21.9 118.7 %all-gather.7.cloned.1.call-done = bf16[2048,2048]{1,0:T(8,128)(2,1)} async-done(((bf16[256,2048]{1,0:T(8,128)(2,1)}), bf16[2048,2048]{1,0:T(8,128)(2,1)}) %all-gather.7.cloned.1.call-update) | async-done | bytes 8388624 | tf_op jit(solution)/shard_map/all_gather | solution.py:198
  224.4 9.4 multiply_bitcast_fusion
  233.7 133.9 %custom-call.14 = f32[2,32,1,64,64]{1,3,4,2,0:T(8,128)} custom-call(f32[2,32,1,64,64]{1,4,3,2,0:T(8,128)} %get-tuple-element.854), custom_call_target="InvertDiagBlocksLowerTriangular" | custom-call | tf_op jit(solution)/shard_map/jvp(vmap())/triangular_solve/custom-call.1 | solution.py:76
  389.3 235.4 %while.40 = (s32[]{:T(128)}, f32[2,128,128]{2,1,0:T(8,128)S(1)}, f32[32,2,64,128]{3,2,0,1:T(8,128)}, f32[32,2,128,128]{3,2,1,0:T(8,128)}, f32[32]{0:T(128)S(1)},...) while((s32[]{:T(128)}, f32[2,128,128]{2,1,0:T(8,128)S(1)}, ...), condition=%wide.region_5.7_spmd.clone, body=%wide.region_4.6_spmd.clone.sunk | while | flops 88358912 | bytes 1512373 | solution.py:110
  640.4 146.7 %reduce-scatter.5.cloned.1.call-done = bf16[256,2048]{1,0:T(8,128)(2,1)} async-done(((bf16[2048,2048]{1,0:T(8,128)(2,1)}), bf16[256,2048]{1,0:T(8,128)(2,1)}) %reduce-scatter.5.cloned.1.call-update) | async-done | bytes 1048592 | tf_op jit(solution)/shard_map/reduce_scatter | solution.py:243
  791.4 123.5 %all-gather.9.cloned.1.call-done = bf16[2048,2048]{1,0:T(8,128)(2,1)} async-done(((bf16[256,2048]{1,0:T(8,128)(2,1)}), bf16[2048,2048]{1,0:T(8,128)(2,1)}) %all-gather.9.cloned.1.call-update) | async-done | bytes 8388624 | tf_op jit(solution)/shard_map/all_gather | solution.py:253
  914.9 11.3 fusion.142
  934.2 106.0 %all-gather.11.cloned.1.call-done = bf16[2048,2048]{1,0:T(8,128)(2,1)} async-done(((bf16[256,2048]{1,0:T(8,128)(2,1)}), bf16[2048,2048]{1,0:T(8,128)(2,1)}) %all-gather.11.cloned.1.call-update) | async-done | bytes 8388624 | tf_op jit(solution)/shard_map/all_gather | solution.py:265
  1040.2 14.7 multiply_convert_fusion
  1054.9 10.7 fusion.143
  1065.6 12.5 add_convert_fusion.1
  1078.2 147.3 %reduce-scatter.9.cloned.1.call-done = bf16[256,2048]{1,0:T(8,128)(2,1)} async-done(((bf16[2048,2048]{1,0:T(8,128)(2,1)}), bf16[256,2048]{1,0:T(8,128)(2,1)}) %reduce-scatter.9.cloned.1.call-update) | async-done | bytes 1048592 | tf_op jit(solution)/shard_map/reduce_scatter | solution.py:274
  1245.1 10.7 convolution_convert_fusion.2
  1255.8 11.0 convolution_convert_fusion.3
  1274.3 82.1 %all-gather.13.cloned.1.call-done = bf16[2048,2048]{1,0:T(8,128)(2,1)} async-done(((bf16[256,2048]{1,0:T(8,128)(2,1)}), bf16[2048,2048]{1,0:T(8,128)(2,1)}) %all-gather.13.cloned.1.call-update) | async-done | bytes 8388624 | tf_op jit(solution)/shard_map/all_gather | solution.py:285
  1382.7 380.1 %while.41 = (s32[]{:T(128)}, f32[2,128,128]{2,1,0:T(8,128)S(1)}, f32[32,2,64,128]{3,2,0,1:T(8,128)}, f32[32,2,64,128]{3,2,0,1:T(8,128)}, f32[32,2,64,128]{3,2,1,...) while((s32[]{:T(128)}, f32[2,128,128]{2,1,0:T(8,128)S(1)}, ...), condition=%wide.region_14.16_spmd.clone, body=%wide.region_13.15_spmd.clone.sunk | while | flops 201637888 | bytes 3902479 | solution.py:110
  1826.9 10.2 fusion.79
  1947.4 26.3 %add_convert_fusion = bf16[2048,2048]{1,0:T(8,128)(2,1)} fusion(f32[2048,2048]{1,0:T(8,128)} %fusion.133, f32[2048,2048]{1,0:T(8,128)} %fusion.151, f32[2048,2048]{1,0:T(8,128)} %fusion.145, f32[2048,2048]{1,0:T(8,128)} %fusion.150, bf16[2048,256]{0,1:T(8,128)(2,1)S(1)} %bitcast.473, bf16[2048,256]{1,0:T(8,128)(2,1)S(1)} %copy-done.65), kind=kOutput, calls=%fused_computation.70 | convolution fusion | flops 2168455168 | bytes 77594624 | tf_op jit(solution)/shard_map/sh,dh->sd/dot_general | solution.py:298
  1974.0 11.2 convolution_convert_fusion
  1989.9 12.5 all-reduce.33
  2011.6 133.9 %all-reduce.37.cloned.1.call-done = (bf16[2048,256]{1,0:T(8,128)(2,1)}, bf16[2048,256]{1,0:T(8,128)(2,1)}, bf16[2048,256]{1,0:T(8,128)(2,1)}, bf16[256,2048]{1,0...) async-done(((bf16[2048,256]{1,0:T(8,128)(2,1)}, bf16[2048,256]{1,0:T(8,128)(2,1)}, bf16[2048,256]{1,0:T(8,128)(2,1)}, ...) | async-done | bytes 12845072 | tf_op jit(solution)/shard_map/psum | solution.py:322
  2164.2 134.3 %reduce-scatter.11.cloned.1.call-done = bf16[256,2048]{1,0:T(8,128)(2,1)} async-done(((bf16[2048,2048]{1,0:T(8,128)(2,1)}), bf16[256,2048]{1,0:T(8,128)(2,1)}) %reduce-scatter.11.cloned.1.call-update) | async-done | bytes 1048592 | tf_op jit(solution)/shard_map/reduce_scatter | solution.py:301
  2300.7 43.0 %all-reduce.32 = (f32[2048]{0:T(1024)}, f32[128]{0:T(128)}, f32[2048]{0:T(1024)}) all-reduce(f32[2048]{0:T(1024)S(1)} %get-tuple-element.718, f32[128]{0:T(128)S(1)} %copy-done.136, f32[2048]{0:T(1024)S(1)} %copy-done.101), channel_id=1, replica_groups=mesh['dp'=4,'tensor'=8] {'dp','tensor'}, use_global_device_ids=true, to_apply=%region_23.27 | all-reduce | flops 4224 | bytes 33792 | tf_op jit(solution)/shard_map/psum | solution.py:306
  2343.7 107.7 %reduce-scatter.7.cloned.1.call-done = bf16[256,2048]{1,0:T(8,128)(2,1)} async-done(((bf16[2048,2048]{1,0:T(8,128)(2,1)}), bf16[256,2048]{1,0:T(8,128)(2,1)}) %reduce-scatter.7.cloned.1.call-update) | async-done | bytes 1048592 | tf_op jit(solution)/shard_map/reduce_scatter | solution.py:259
  (1260 shorter events, 1028.2 us)
Async XLA Ops:
  7.2 1033.0 %copy-start = (bf16[704,2048]{1,0:T(8,128)(2,1)S(1)}, bf16[704,2048]{1,0:T(8,128)(2,1)}, u32[]{:S(2)}) copy-start(bf16[704,2048]{1,0:T(8,128)(2,1)} %param.44) | copy-start | bytes 8650756
  7.2 133.3 %all-gather.7.cloned.1.call-start = ((), (), s32[]{:S(2)}) async-start(), calls=%async_computation.4 | async-start | bytes 9437184 | tf_op jit(solution)/shard_map/all_gather | solution.py:198
  12.8 774.3 %reduce-scatter.5.cloned.1.call-start = ((), (), s32[]{:S(2)}) async-start(), calls=%async_computation.5 | async-start | bytes 9437184 | tf_op jit(solution)/shard_map/reduce_scatter | solution.py:243
  19.5 204.8 %copy-start.75 = (f32[64,64]{1,0:T(8,128)}, f32[64,64]{1,0:T(8,128)S(1)}, u32[]{:S(2)}) copy-start(f32[64,64]{1,0:T(8,128)S(1)} %fusion.110) | copy-start | bytes 49156
  19.5 204.8 %copy-start.79 = (f32[64,64]{1,0:T(8,128)}, f32[64,64]{1,0:T(8,128)S(1)}, u32[]{:S(2)}) copy-start(f32[64,64]{1,0:T(8,128)S(1)} %fusion.109) | copy-start | bytes 49156
  20.0 164.0 %copy-start.122 = (f32[1,256]{1,0:T(1,128)}, f32[1,256]{1,0:T(1,128)S(1)}, u32[]{:S(2)}) copy-start(f32[1,256]{1,0:T(1,128)S(1)} %get-tuple-element.878) | copy-start | bytes 3076
  20.0 164.0 %copy-start.124 = (f32[1,256]{1,0:T(1,128)}, f32[1,256]{1,0:T(1,128)S(1)}, u32[]{:S(2)}) copy-start(f32[1,256]{1,0:T(1,128)S(1)} %get-tuple-element.880) | copy-start | bytes 3076
  20.0 164.0 %copy-start.126 = (f32[1,256]{1,0:T(1,128)}, f32[1,256]{1,0:T(1,128)S(1)}, u32[]{:S(2)}) copy-start(f32[1,256]{1,0:T(1,128)S(1)} %get-tuple-element.879) | copy-start | bytes 3076
  20.0 164.0 %copy-start.128 = (f32[1,256]{1,0:T(1,128)}, f32[1,256]{1,0:T(1,128)S(1)}, u32[]{:S(2)}) copy-start(f32[1,256]{1,0:T(1,128)S(1)} %get-tuple-element.881) | copy-start | bytes 3076
  20.2 204.1 %copy-start.97 = (pred[64,64]{1,0:T(8,128)(4,1)}, pred[64,64]{1,0:T(8,128)(4,1)S(1)}, u32[]{:S(2)}) copy-start(pred[64,64]{1,0:T(8,128)(4,1)S(1)} %iota_compare_fusion.1) | copy-start | bytes 12292
  146.9 230.7 %copy-start.63 = (f32[2,32,64]{2,1,0:T(8,128)}, f32[2,32,64]{2,1,0:T(8,128)S(1)}, u32[]{:S(2)}) copy-start(f32[2,32,64]{2,1,0:T(8,128)S(1)} %mul.1002) | copy-start | bytes 49156
  639.8 275.1 %all-gather.9.cloned.1.call-start = ((), (), s32[]{:S(2)}) async-start(), calls=%async_computation.6 | async-start | bytes 9437184 | tf_op jit(solution)/shard_map/all_gather | solution.py:253
  640.4 588.5 %copy-start.81 = (f32[2048]{0:T(1024)}, f32[2048]{0:T(1024)S(1)}, u32[]{:S(2)}) copy-start(f32[2048]{0:T(1024)S(1)} %convert_element_type.276) | copy-start | bytes 24580
  789.3 439.6 %copy-start.102 = (f32[256]{0:T(256)}, f32[256]{0:T(256)S(1)}, u32[]{:S(2)}) copy-start(f32[256]{0:T(256)S(1)} %add_rsqrt_fusion.2) | copy-start | bytes 3076
  790.8 249.4 %all-gather.11.cloned.1.call-start = ((), (), s32[]{:S(2)}) async-start(), calls=%async_computation.8 | async-start | bytes 9437184 | tf_op jit(solution)/shard_map/all_gather | solution.py:265
  791.4 434.2 %reduce-scatter.9.cloned.1.call-start = ((), (), s32[]{:S(2)}) async-start(), calls=%async_computation.9 | async-start | bytes 9437184 | tf_op jit(solution)/shard_map/reduce_scatter | solution.py:274
  1078.1 278.2 %all-gather.13.cloned.1.call-start = ((), (), s32[]{:S(2)}) async-start(), calls=%async_computation.10 | async-start | bytes 9437184 | tf_op jit(solution)/shard_map/all_gather | solution.py:285
  1232.3 772.6 %all-gather.15.cloned.1.call-start = ((), (), s32[]{:S(2)}) async-start(), calls=%async_computation.12 | async-start | bytes 5242880 | tf_op jit(solution)/shard_map/all_gather | solution.py:11
  1881.0 264.6 %all-reduce.37.cloned.1.call-start = ((), (), s32[]{:S(2)}) async-start(), calls=%async_computation.13 | async-start | bytes 25690112 | tf_op jit(solution)/shard_map/psum | solution.py:322
  1913.8 384.6 %reduce-scatter.11.cloned.1.call-start = ((), (), s32[]{:S(2)}) async-start(), calls=%async_computation.11 | async-start | bytes 9437184 | tf_op jit(solution)/shard_map/reduce_scatter | solution.py:301
  1973.7 477.7 %reduce-scatter.7.cloned.1.call-start = ((), (), s32[]{:S(2)}) async-start(), calls=%async_computation.7 | async-start | bytes 9437184 | tf_op jit(solution)/shard_map/reduce_scatter | solution.py:259
  2164.1 287.2 %copy-start.82 = (f32[2048]{0:T(1024)S(1)}, f32[2048]{0:T(1024)}, u32[]{:S(2)}) copy-start(f32[2048]{0:T(1024)} %copy-done.81) | copy-start | bytes 24580
  2164.1 287.2 %copy-start.103 = (f32[256]{0:T(256)S(1)}, f32[256]{0:T(256)}, u32[]{:S(2)}) copy-start(f32[256]{0:T(256)} %copy-done.102) | copy-start | bytes 3076
  2164.2 287.2 %copy-start.107 = (f32[256]{0:T(256)S(1)}, f32[256]{0:T(256)}, u32[]{:S(2)}) copy-start(f32[256]{0:T(256)} %copy-done.106) | copy-start | bytes 3076
  (140 other events, 3092.8 us)
Sparse Core Ops, SparseCore 0:
  12.9 127.6 all-gather.6
  639.9 147.1 reduce-scatter.4
  790.9 123.9 all-gather.8
  917.1 123.1 all-gather.10
  1078.3 147.2 reduce-scatter.8
  1232.4 123.9 all-gather.12
  1881.1 32.6 all-gather.14
  1918.2 227.3 all-reduce.36
  2149.2 149.1 reduce-scatter.10
  2302.4 148.9 reduce-scatter.6
